TPU v7x, 32 devices: a whole 2x2x4 slice. The times are simulated.
32 devices in a mesh: dp: 4 (over x, core), ctx: 2 (over y), head: 4 (over z).
Axes of the slice: x: 2, y: 2, z: 4, core: 2. Of those that a mesh axis runs over, the one named last changes fastest.
Arguments:
- inputs: bfloat16 [16, 256, 1024], P('dp', 'ctx', 'head'), parts along dimension 0, may hold values from -6 to 6
- lengths: int32 [16], P('dp'), parts along dimension 0, may hold values from 1 to 640, 1024 in all
- proj_in: bfloat16 [1024, 4, 1024], P(None, None, 'head'), may hold values from -0.1875 to 0.1875
- proj_out: bfloat16 [1024, 1024], P('head'), may hold values from -0.1875 to 0.1875
Outputs:
- layer_out: bfloat16 [8, 2, 256, 1024], P(('dp', 'ctx'), None, None, 'head'), parts along dimension 0
There are 4 independent parts, one for each index of `dp`. A program takes and returns all parts, laid end to end along the dimension named above; an argument that names none is the same for every part. Nothing has to cross between parts.
Inputs may be any that keep to these rules, and one draw needn't show every extreme that they name: The 4 histories lie end to end in the packed rows; the lengths sum to 1024 and the longest is exactly 640.
All inputs are finite; a program needn't handle non-finite values.
Results may differ from a plain program's by a relative error of at most 0.0055.
Values may be sent and summed in bfloat16 or wider, within the bound.
No kernel may reach another device: no remote copies, remote signals or barrier semaphores. Data moves between devices by JAX's collectives and lax.ppermute only.
A program may use at most 64 MiB of HBM per device.

v0:
```python
import math
import jax
import jax.numpy as jnp
from jax import lax
from jax.sharding import PartitionSpec as P

HDIM = 128


def layer_norm(values, epsilon):
    center = values - jnp.mean(values, axis=-1, keepdims=True)
    spread = jnp.mean(center * center, axis=-1, keepdims=True)
    return center * lax.rsqrt(spread + epsilon)


def silu_round(values):
    return jax.nn.silu(values).astype(jnp.bfloat16)


def body(inputs, lengths, proj_in, proj_out):
    context_size = lax.axis_size("ctx")
    own_index = lax.axis_index("ctx")
    block_total, stripe, width_part = inputs.shape
    block_len = stripe * context_size
    row_count = 2 * block_len
    heads_dev = proj_in.shape[2] // HDIM
    reordered = jnp.stack([inputs[:context_size], inputs[context_size:][::-1]], axis=1)
    reordered = reordered.reshape(block_total, stripe, width_part)
    own_rows = lax.all_to_all(reordered, "ctx", split_axis=0, concat_axis=1, tiled=True)
    full_rows = lax.all_gather(own_rows, "head", axis=2, tiled=True)
    normed = layer_norm(full_rows.reshape(row_count, -1).astype(jnp.float32), 1e-06).astype(
        jnp.bfloat16
    )
    user_ends = jnp.cumsum(lengths)

    def segment(position):
        return jnp.sum((position[:, None] >= user_ends[None, :]).astype(jnp.int32), axis=1)

    offsets = jnp.arange(block_len, dtype=jnp.int32)
    own_blocks = jnp.stack([own_index, 2 * context_size - 1 - own_index])
    query_pos = (own_blocks[:, None] * block_len + offsets[None, :]).reshape(-1)
    query_seg = segment(query_pos)
    score_scale = 1.0 / math.sqrt(HDIM)
    projected = silu_round(
        jnp.einsum("rd,dgc->rgc", normed, proj_in, preferred_element_type=jnp.float32)
    )
    gating = projected[:, 0]
    queries = projected[:, 2]
    key_pair = (
        projected[:, 3].reshape(2, block_len, -1),
        projected[:, 1].reshape(2, block_len, -1),
    )

    def loader(shards, lead_row, tile_rows):
        key_rows = lax.dynamic_slice_in_dim(shards[0], lead_row, tile_rows, 0)
        value_rows = lax.dynamic_slice_in_dim(shards[1], lead_row, tile_rows, 0)
        return (
            key_rows.reshape(tile_rows * block_len, heads_dev, HDIM),
            value_rows.reshape(tile_rows * block_len, heads_dev, HDIM),
        )

    query_heads = queries.reshape(row_count, heads_dev, HDIM)
    zero_acc = jnp.zeros((row_count, heads_dev, HDIM), jnp.float32)
    shards = (
        lax.all_gather(key_pair[0], "ctx", axis=0, tiled=True),
        lax.all_gather(key_pair[1], "ctx", axis=0, tiled=True),
    )
    piece_rows = shards[0].shape[0]
    tile_rows = 4

    def one_tile(tile_index, partial_value):
        lead_row = tile_index * tile_rows
        listed = lead_row + jnp.arange(tile_rows, dtype=jnp.int32)
        holder = listed // 2
        block_ids = jnp.where(listed % 2 == 0, holder, 2 * context_size - 1 - holder)
        key_pos = (block_ids[:, None] * block_len + offsets[None, :]).reshape(-1)
        allowed = (query_seg[:, None] == segment(key_pos)[None, :]) & (
            key_pos[None, :] <= query_pos[:, None]
        )
        key_rows, value_rows = loader(shards, lead_row, tile_rows)
        scores = (
            jnp.einsum("qhd,khd->hqk", query_heads, key_rows, preferred_element_type=jnp.float32)
            * score_scale
        )
        weights = jnp.where(allowed[None], jax.nn.silu(scores), 0.0).astype(jnp.bfloat16)
        return partial_value + jnp.einsum(
            "hqk,khd->qhd", weights, value_rows, preferred_element_type=jnp.float32
        )

    attended = lax.fori_loop(0, piece_rows // tile_rows, one_tile, zero_acc)
    gate_prod = layer_norm(attended, 1e-05) * gating.reshape(row_count, heads_dev, HDIM).astype(
        jnp.float32
    )
    gate_prod = gate_prod.astype(jnp.bfloat16).reshape(row_count, -1)
    columns = lax.all_to_all(proj_out, "head", split_axis=1, concat_axis=0, tiled=True)
    summed = jnp.dot(
        lax.all_gather(gate_prod, "head", axis=1, tiled=True),
        columns,
        preferred_element_type=jnp.float32,
    )
    result = (own_rows.reshape(row_count, -1).astype(jnp.float32) + summed).astype(jnp.bfloat16)
    return result.reshape(1, 2, block_len, -1)


def solution(mesh):
    return jax.shard_map(
        body,
        mesh=mesh,
        in_specs=(P("dp", "ctx", "head"), P("dp"), P(None, None, "head"), P("head", None)),
        out_specs=P(("dp", "ctx"), None, None, "head"),
        check_vma=False,
    )
```

profile of v0, /device:TPU:0, one launch (start us, length us, event | category | flops | bytes accessed | tf_op | source)
XLA Modules:
  0.0 122.5 jit_solution(3696694843933152079)
XLA Ops:
  6.5 1.1 slice_bitcast_fusion
  7.7 9.2 %all_to_all.37 = bf16[4,128,256]{2,1,0:T(8,128)(2,1)S(1)} all-to-all(bf16[4,128,256]{2,1,0:T(8,128)(2,1)S(1)} %bitcast.59), channel_id=1, replica_groups=mesh['dp'=4,'ctx'=2,'head'=4] {'ctx'}, dimensions={0} | all-to-all | bytes 524288 | tf_op jit(solution)/shard_map/all_to_all | solution.py:29
  17.0 0.7 copy.34
  17.7 0.0 all-gather.5.cloned.1.call-start
  17.8 0.1 add_multiply_fusion
  17.9 0.1 add_bitcast_fusion.1
  17.9 0.1 add_bitcast_fusion
  18.0 0.2 reduce-window.8
  18.2 0.1 convert_reduce_fusion.2
  18.3 0.1 convert_reduce_fusion.1
  18.4 1.3 %compare_and_fusion = pred[512,1024]{1,0:T(8,128)(4,1)} fusion(s32[1024]{0:T(1024)S(1)} %bitcast.63, s32[1024]{0:T(1024)S(1)} %convert_reduce_fusion.1, s32[512]{0:T(512)S(1)} %bitcast.65, s32[512]{0:T(512)S(1)} %convert_reduce_fusion.2), kind=kLoop, calls=%fused_computation.8 | loop fusion | flops 1572864 | bytes 536576 | tf_op jit(solution)/shard_map/while/body/eval_jaxpr/and | solution.py:77
  19.7 28.5 %all-gather.3.cloned.1.call-done = bf16[2,256,1024]{2,1,0:T(8,128)(2,1)} async-done(((bf16[2,256,256]{2,1,0:T(8,128)(2,1)}), bf16[2,256,1024]{2,1,0:T(8,128)(2,1)}) %all-gather.3.cloned.1.call-update) | async-done | bytes 1048592 | tf_op jit(solution)/shard_map/all_gather | solution.py:30
  48.2 1.5 %convert_reduce_fusion = f32[2,256]{1,0:T(2,128)S(1)} fusion(bf16[2,256,1024]{2,1,0:T(8,128)(2,1)} %all-gather.3.cloned.1.call-done), kind=kLoop, calls=%fused_computation.14 | loop fusion | flops 1048064 | bytes 1050624 | tf_op jit(solution)/shard_map/reduce_sum | solution.py:11
  49.7 1.6 %multiply_reduce_fusion = f32[2,256]{1,0:T(2,128)S(1)} fusion(bf16[2,256,1024]{2,1,0:T(8,128)(2,1)} %all-gather.3.cloned.1.call-done, f32[2,256]{1,0:T(2,128)S(1)} %get-tuple-element.40), kind=kLoop, calls=%fused_computation.7 | loop fusion | flops 2096640 | bytes 1052672 | tf_op jit(solution)/shard_map/reduce_sum | solution.py:12
  51.4 0.3 fusion.1
  51.7 1.5 %multiply_convert_fusion = bf16[512,4,256]{2,0,1:T(8,128)(2,1)S(1)} fusion(bf16[1024,4,256]{2,1,0:T(4,128)(2,1)S(1)} %copy-done, bf16[512,1024]{1,0:T(8,128)(2,1)S(1)} %fusion.1), kind=kOutput, calls=%fused_computation.6 | convolution fusion | flops 1076363264 | bytes 4194304 | tf_op jit(solution)/shard_map/rd,dgc->rgc/dot_general | solution.py:45
  53.2 0.9 fusion.22
  54.1 7.7 %all_gather.14 = bf16[4,256,256]{2,1,0:T(8,128)(2,1)S(1)} all-gather(bf16[2,256,256]{2,1,0:T(8,128)(2,1)S(1)} %bitcast.56), channel_id=1, replica_groups=mesh['dp'=4,'ctx'=2,'head'=4] {'ctx'}, dimensions={0}, use_global_device_ids=true | all-gather | bytes 786432 | tf_op jit(solution)/shard_map/all_gather | solution.py:65
  61.8 0.9 reshape.244
  62.7 7.9 %all_gather.13 = bf16[4,256,256]{2,1,0:T(8,128)(2,1)S(1)} all-gather(bf16[2,256,256]{2,1,0:T(8,128)(2,1)S(1)} %bitcast.55), channel_id=1, replica_groups=mesh['dp'=4,'ctx'=2,'head'=4] {'ctx'}, dimensions={0}, use_global_device_ids=true | all-gather | bytes 786432 | tf_op jit(solution)/shard_map/all_gather | solution.py:66
  70.6 0.9 reshape.251
  71.5 0.1 reshape_squeeze.11
  71.6 3.5 %fusion.23 = (f32[512,2]{0,1:T(2,128)S(1)}, f32[512,2,128]{0,2,1:T(8,128)S(1)}) fusion(pred[512,1024]{1,0:T(8,128)(4,1)} %compare_and_fusion, bf16[1024,2,128]{2,1,0:T(2,128)(2,1)} %reshape.244, bf16[512,2,128]{2,1,0:T(2,128)(2,1)S(1)} %reshape_squeeze.11, bf16[1024,2,128]{2,1,0:T(2,128)(2,1)} %reshape.251), kind=kOutput, calls=%fused_computation.45 | convolution fusion | flops 544340992 | bytes 2363392 | tf_op jit(solution)/shard_map/while/body/eval_jaxpr/hqk,khd->qhd/dot_general | solution.py:86
  75.1 0.1 multiply_reduce_fusion.1
  75.2 1.2 %copy.43 = f32[512,1,256]{0,2,1:T(8,128)S(1)} copy(f32[512,1,256]{2,0,1:T(8,128)} %get-tuple-element.24) | data formatting | bytes 1048576 | tf_op jit(solution)/shard_map/convert_element_type | solution.py:91
  76.5 0.8 multiply_convert_fusion.1
  77.3 2.1 %copy.40 = bf16[256,1024]{0,1:T(8,128)(2,1)} copy(bf16[256,1024]{1,0:T(8,128)(2,1)} %param.7) | data formatting | bytes 1048576 | tf_op args[3]
  79.4 3.5 %all-to-all-start.1 = ((bf16[256,4,256]{0,2,1:T(8,128)(2,1)}), bf16[256,4,256]{0,2,1:T(8,128)(2,1)S(1)}, u32[]{:S(2)}, u32[]{:S(2)}) async-start(bf16[256,4,256]{0,2,1:T(8,128)(2,1)} %bitcast.19), calls=%async_computation.1 | async-start | bytes 1048576 | tf_op jit(solution)/shard_map/all_to_all | solution.py:95
  82.9 25.4 %all-to-all-done.1 = bf16[256,4,256]{0,2,1:T(8,128)(2,1)S(1)} async-done(((bf16[256,4,256]{0,2,1:T(8,128)(2,1)}), bf16[256,4,256]{0,2,1:T(8,128)(2,1)S(1)}, u32[]{:S(2)}, u32[]{:S(2)}) %all-to-all-start.1) | async-done | bytes 524320 | tf_op jit(solution)/shard_map/all_to_all | solution.py:95
  108.4 1.0 copy.41
  109.4 3.7 %all-gather.5.cloned.1.call-done = bf16[512,1024]{0,1:T(8,128)(2,1)} async-done(((bf16[512,256]{0,1:T(8,128)(2,1)}), bf16[512,1024]{0,1:T(8,128)(2,1)}) %all-gather.5.cloned.1.call-update) | async-done | bytes 1048592 | tf_op jit(solution)/shard_map/all_gather | solution.py:97
  113.1 2.5 %fusion.6 = bf16[512,256]{1,0:T(8,128)(2,1)} fusion(f32[512,256]{1,0:T(8,128)S(1)} %bitcast.60, bf16[512,1024]{0,1:T(8,128)(2,1)} %all-gather.5.cloned.1.call-done, bf16[1024,256]{1,0:T(8,128)(2,1)} %bitcast.61), kind=kOutput, calls=%fused_computation.12 | convolution fusion | flops 268697600 | bytes 2359296 | tf_op jit(solution)/shard_map/dot_general | solution.py:96
  (21 shorter events, 0.2 us)
Async XLA Ops:
  6.5 45.2 %copy-start = (bf16[1024,4,256]{2,1,0:T(4,128)(2,1)S(1)}, bf16[1024,4,256]{2,1,0:T(4,128)(2,1)}, u32[]{:S(2)}) copy-start(bf16[1024,4,256]{2,1,0:T(4,128)(2,1)} %param.6) | copy-start | bytes 6291460
  6.5 11.5 %copy-start.2 = (s32[4]{0:T(128)S(1)}, s32[4]{0:T(128)}, u32[]{:S(2)}) copy-start(s32[4]{0:T(128)} %param.5) | copy-start | bytes 52
  6.5 41.6 %all-gather.3.cloned.1.call-start = ((), (), s32[]{:S(2)}) async-start(), calls=%async_computation.2 | async-start | bytes 1310720 | tf_op jit(solution)/shard_map/all_gather | solution.py:30
  17.7 95.4 %all-gather.5.cloned.1.call-start = ((), (), s32[]{:S(2)}) async-start(), calls=%async_computation.3 | async-start | bytes 1310720 | tf_op jit(solution)/shard_map/all_gather | solution.py:97
  48.2 3.2 %copy-start.1 = (bf16[2,256,1024]{2,1,0:T(8,128)(2,1)S(1)}, bf16[2,256,1024]{2,1,0:T(8,128)(2,1)}, u32[]{:S(2)}) copy-start(bf16[2,256,1024]{2,1,0:T(8,128)(2,1)} %all-gather.3.cloned.1.call-done) | copy-start | bytes 3145732
  79.4 29.0 %all-to-all-start.1 = ((bf16[256,4,256]{0,2,1:T(8,128)(2,1)}), bf16[256,4,256]{0,2,1:T(8,128)(2,1)S(1)}, u32[]{:S(2)}, u32[]{:S(2)}) async-start(bf16[256,4,256]{0,2,1:T(8,128)(2,1)} %bitcast.19), calls=%async_computation.1 | async-start | bytes 1048576 | tf_op jit(solution)/shard_map/all_to_all | solution.py:95
Sparse Core Ops, SparseCore 0:
  17.8 30.2 all-gather.2
  77.4 35.6 all-gather.4
where the time goes:
time: 123 us; the launch traced here: 122 us
  waiting for transfers between devices  57.7 us (47%)
  blocking collectives  24.8 us (20%)
  between operations  13.5 us (11%)
  local copies, waits for them, and re-layouts  8.2 us (7%)
  matrix products  7.57 us (6%)
  other arithmetic  7.19 us (6%)
  starting transfers between devices  3.51 us (3%)
    all_gather x1, waiting for transfers between devices, body(): full_rows = lax.all_gather(own_rows, 'head', axis=2, tiled=True)  28.5 us
    all_to_all x1, waiting for transfers between devices, body(): lax.all_to_all(proj_out, 'head', split_axis=1, concat_axis=0, tiled=True)  25.4 us
    all_to_all x1, blocking collectives, body(): lax.all_to_all(reordered, 'ctx', split_axis=0, concat_axis=1, tiled=True)  9.24 us
    all_gather x1, blocking collectives, body(): lax.all_gather(key_pair[1], 'ctx', axis=0, tiled=True)  7.86 us
    all_gather x1, blocking collectives, body(): lax.all_gather(key_pair[0], 'ctx', axis=0, tiled=True)  7.68 us
    all_gather x1, waiting for transfers between devices, body(): lax.all_gather(gate_prod, 'head', axis=1, tiled=True)  3.71 us
    dot_general x1, matrix products, one_tile(): jnp.einsum('hqk,khd->qhd', weights, value_rows, preferred_element_type=jn...  3.53 us
    all_to_all x1, starting transfers between devices, body(): lax.all_to_all(proj_out, 'head', split_axis=1, concat_axis=0, tiled=True)  3.47 us
  transfers between devices with their start and end apart: 3, of which 3 were waited for; matrix products, arithmetic and copies ran while one was open for 4% of the time, Pallas kernels for 0%

commit v1 on v0

--- a/solution.py
+++ b/solution.py
@@ -27,7 +27,23 @@
     reordered = jnp.stack([inputs[:context_size], inputs[context_size:][::-1]], axis=1)
     reordered = reordered.reshape(block_total, stripe, width_part)
     own_rows = lax.all_to_all(reordered, "ctx", split_axis=0, concat_axis=1, tiled=True)
-    full_rows = lax.all_gather(own_rows, "head", axis=2, tiled=True)
+    ways, here, hop = (lax.axis_size("head"), lax.axis_index("head"), own_rows.shape[2])
+    shape = [n * ways if d == 2 else n for d, n in enumerate(own_rows.shape)]
+    full = lax.dynamic_update_slice_in_dim(
+        jnp.zeros(shape, own_rows.dtype), own_rows, here * hop, axis=2
+    )
+    going_up = going_down = own_rows
+    for far in range(1, ways // 2 + 1):
+        going_up = lax.ppermute(going_up, "head", [(d, (d + 1) % ways) for d in range(ways)])
+        full = lax.dynamic_update_slice_in_dim(full, going_up, (here - far) % ways * hop, axis=2)
+        if 2 * far < ways:
+            going_down = lax.ppermute(
+                going_down, "head", [(d, (d - 1) % ways) for d in range(ways)]
+            )
+            full = lax.dynamic_update_slice_in_dim(
+                full, going_down, (here + far) % ways * hop, axis=2
+            )
+    full_rows = full
     normed = layer_norm(full_rows.reshape(row_count, -1).astype(jnp.float32), 1e-06).astype(
         jnp.bfloat16
     )

time: 123 us -> 107 us (0.87)
  waiting for transfers between devices: 57.7 us -> 44.7 us
  blocking collectives: 24.8 us -> 14.1 us
  starting transfers between devices: 3.51 us -> 13.2 us
    all_gather x1 -> x0, waiting for transfers between devices: 28.5 us -> none  [body(): full_rows = lax.all_gather(own_rows, 'head', axis=2, tiled=True)]
    ppermute x0 -> x3, waiting for transfers between devices: none -> 13.6 us  [the longest x2 10.7 us: body(): lax.ppermute(going_up, 'head', [(d, (d + 1) % ways) for d in range(ways)])]
    all_to_all x1 -> x0, blocking collectives: 9.24 us -> none  [body(): lax.all_to_all(reordered, 'ctx', split_axis=0, concat_axis=1, tiled=True)]
    ppermute x0 -> x3, starting transfers between devices: none -> 5.42 us  [the longest x2 3.38 us: body(): lax.ppermute(going_up, 'head', [(d, (d + 1) % ways) for d in range(ways)])]
    all_to_all x0 -> x1, waiting for transfers between devices: none -> 4.72 us  [body(): lax.all_to_all(reordered, 'ctx', split_axis=0, concat_axis=1, tiled=True)]
    all_to_all x0 -> x1, starting transfers between devices: none -> 4.26 us  [body(): lax.all_to_all(reordered, 'ctx', split_axis=0, concat_axis=1, tiled=True)]
    all_to_all x1, waiting for transfers between devices: 25.4 us -> 22 us  [body(): lax.all_to_all(proj_out, 'head', split_axis=1, concat_axis=0, tiled=True)]
    reduce_sum x1, other arithmetic: 1.52 us -> 0.21 us  [layer_norm(): center = values - jnp.mean(values, axis=-1, keepdims=True)]
  transfers between devices with their start and end apart: 3 -> 6, of which waited for: 3 -> 6; matrix products, arithmetic and copies ran while one was open for 4% -> 5% of each run, Pallas kernels for 0% -> 0%
where the time goes in v1:
time: 107 us
  waiting for transfers between devices  44.7 us (42%)
  blocking collectives  14.1 us (13%)
  between operations  13.5 us (13%)
  starting transfers between devices  13.2 us (12%)
  local copies, waits for them, and re-layouts  7.71 us (7%)
  matrix products  7.58 us (7%)
  other arithmetic  6 us (6%)
    all_to_all x1, waiting for transfers between devices, body(): lax.all_to_all(proj_out, 'head', split_axis=1, concat_axis=0, tiled=True)  22 us
    ppermute x2, waiting for transfers between devices, body(): lax.ppermute(going_up, 'head', [(d, (d + 1) % ways) for d in range(ways)])  10.7 us
    all_gather x1, blocking collectives, body(): lax.all_gather(key_pair[0], 'ctx', axis=0, tiled=True)  7.03 us
    all_gather x1, blocking collectives, body(): lax.all_gather(key_pair[1], 'ctx', axis=0, tiled=True)  7.03 us
    all_to_all x1, waiting for transfers between devices, body(): lax.all_to_all(reordered, 'ctx', split_axis=0, concat_axis=1, tiled=True)  4.72 us
    all_gather x1, waiting for transfers between devices, body(): lax.all_gather(gate_prod, 'head', axis=1, tiled=True)  4.34 us
    all_to_all x1, starting transfers between devices, body(): lax.all_to_all(reordered, 'ctx', split_axis=0, concat_axis=1, tiled=True)  4.26 us
    dot_general x1, matrix products, one_tile(): jnp.einsum('hqk,khd->qhd', weights, value_rows, preferred_element_type=jn...  3.54 us
  transfers between devices with their start and end apart: 6, of which 6 were waited for; matrix products, arithmetic and copies ran while one was open for 5% of the time, Pallas kernels for 0%

profile of v1, /device:TPU:0, one launch (start us, length us, event | category | flops | bytes accessed | tf_op | source)
XLA Modules:
  0.0 106.7 jit_solution(16951041970413681814)
XLA Ops:
  6.5 1.1 %slice_bitcast_fusion = (bf16[2,1,128,256]{3,2,1,0:T(8,128)(2,1)S(1)}, bf16[2,128,256]{2,1,0:T(8,128)(2,1)S(1)}) fusion(bf16[4,128,256]{2,1,0:T(8,128)(2,1)} %param.4), kind=kLoop, calls=%fused_computation.23 | loop fusion | bytes 524288 | tf_op jit(solution)/shard_map/stack | solution.py:27
  7.7 0.7 pad_maximum_fusion
  8.4 4.3 %all-to-all-start = ((bf16[4,128,256]{2,1,0:T(8,128)(2,1)}), bf16[4,128,256]{2,1,0:T(8,128)(2,1)S(1)}, u32[]{:S(2)}, u32[]{:S(2)}) async-start(bf16[4,128,256]{2,1,0:T(8,128)(2,1)} %bitcast.2), calls=%async_computation | async-start | bytes 524288 | tf_op jit(solution)/shard_map/all_to_all | solution.py:29
  12.9 0.8 reduce-window.8
  13.8 4.7 %all-to-all-done = bf16[4,128,256]{2,1,0:T(8,128)(2,1)S(1)} async-done(((bf16[4,128,256]{2,1,0:T(8,128)(2,1)}), bf16[4,128,256]{2,1,0:T(8,128)(2,1)S(1)}, u32[]{:S(2)}, u32[]{:S(2)}) %all-to-all-start) | async-done | bytes 262176 | tf_op jit(solution)/shard_map/all_to_all | solution.py:29
  18.6 1.8 %collective-permute-start = (bf16[2,256,256]{2,1,0:T(8,128)(2,1)S(1)}, bf16[2,256,256]{2,1,0:T(8,128)(2,1)S(1)}, u32[]{:S(2)}, u32[]{:S(2)}) collective-permute-start(bf16[2,256,256]{2,1,0:T(8,128)(2,1)S(1)} %bitcast.58), channel_id=1, source_target_pairs={{0,1},{1,2},{2,3},{3,0},{4,5},{5,6},{6,7},{7,4},{8,9},{9,10},{10,1... | collective-permute-start | bytes 786440 | tf_op jit(solution)/shard_map/ppermute | solution.py:37
  20.4 0.1 convert_reduce_fusion.2
  20.5 2.0 %collective-permute-start.1 = (bf16[2,256,256]{2,1,0:T(8,128)(2,1)S(1)}, bf16[2,256,256]{2,1,0:T(8,128)(2,1)S(1)}, u32[]{:S(2)}, u32[]{:S(2)}) collective-permute-start(bf16[2,256,256]{2,1,0:T(8,128)(2,1)S(1)} %bitcast.59), channel_id=1, source_target_pairs={{0,3},{1,0},{2,1},{3,2},{4,7},{5,4},{6,5},{7,6},{8,11},{9,8},{10,9... | collective-permute-start | bytes 786440 | tf_op jit(solution)/shard_map/ppermute | solution.py:40
  22.6 1.3 %compare_and_fusion = pred[512,1024]{1,0:T(8,128)(4,1)} fusion(s32[1024]{0:T(1024)S(1)} %bitcast.64, s32[1024]{0:T(1024)S(1)} %convert_reduce_fusion.1, s32[512]{0:T(512)S(1)} %bitcast.66, s32[512]{0:T(512)S(1)} %convert_reduce_fusion.2), kind=kLoop, calls=%fused_computation.8 | loop fusion | flops 1572864 | bytes 536576 | tf_op jit(solution)/shard_map/while/body/eval_jaxpr/and | solution.py:93
  23.9 5.8 %collective-permute-done = bf16[2,256,256]{2,1,0:T(8,128)(2,1)S(1)} collective-permute-done((bf16[2,256,256]{2,1,0:T(8,128)(2,1)S(1)}, bf16[2,256,256]{2,1,0:T(8,128)(2,1)S(1)}, u32[]{:S(2)}, u32[]{:S(2)}) %collective-permute-start) | collective-permute-done | bytes 262176 | tf_op jit(solution)/shard_map/ppermute | solution.py:37
  29.7 1.5 %collective-permute-start.2 = (bf16[2,256,256]{2,1,0:T(8,128)(2,1)S(1)}, bf16[2,256,256]{2,1,0:T(8,128)(2,1)S(1)}, u32[]{:S(2)}, u32[]{:S(2)}) collective-permute-start(bf16[2,256,256]{2,1,0:T(8,128)(2,1)S(1)} %collective-permute-done), channel_id=1, source_target_pairs={{0,1},{1,2},{2,3},{3,0},{4,5},{5,6},{6,7},{7,4},{8,9},{9,10},{10,1... | collective-permute-start | bytes 786440 | tf_op jit(solution)/shard_map/ppermute | solution.py:37
  31.2 0.1 broadcast_in_dim.39
  31.4 2.8 %collective-permute-done.1 = bf16[2,256,256]{2,1,0:T(8,128)(2,1)S(1)} collective-permute-done((bf16[2,256,256]{2,1,0:T(8,128)(2,1)S(1)}, bf16[2,256,256]{2,1,0:T(8,128)(2,1)S(1)}, u32[]{:S(2)}, u32[]{:S(2)}) %collective-permute-start.1) | collective-permute-done | bytes 262176 | tf_op jit(solution)/shard_map/ppermute | solution.py:40
  34.3 4.9 %collective-permute-done.2 = bf16[2,256,256]{2,1,0:T(8,128)(2,1)S(1)} collective-permute-done((bf16[2,256,256]{2,1,0:T(8,128)(2,1)S(1)}, bf16[2,256,256]{2,1,0:T(8,128)(2,1)S(1)}, u32[]{:S(2)}, u32[]{:S(2)}) %collective-permute-start.2) | collective-permute-done | bytes 262176 | tf_op jit(solution)/shard_map/ppermute | solution.py:37
  39.2 0.2 convert_reduce_fusion
  39.4 0.4 multiply_reduce_fusion
  39.9 0.3 fusion.1
  40.2 1.5 %multiply_convert_fusion = bf16[512,4,256]{2,0,1:T(8,128)(2,1)S(1)} fusion(bf16[1024,4,256]{2,1,0:T(4,128)(2,1)S(1)} %copy-done, bf16[512,1024]{1,0:T(8,128)(2,1)S(1)} %fusion.1), kind=kOutput, calls=%fused_computation.6 | convolution fusion | flops 1076363264 | bytes 4194304 | tf_op jit(solution)/shard_map/rd,dgc->rgc/dot_general | solution.py:61
  41.7 0.9 fusion.22
  42.6 7.0 %all_gather.10 = bf16[4,256,256]{2,1,0:T(8,128)(2,1)S(1)} all-gather(bf16[2,256,256]{2,1,0:T(8,128)(2,1)S(1)} %bitcast.56), channel_id=1, replica_groups=mesh['dp'=4,'ctx'=2,'head'=4] {'ctx'}, dimensions={0}, use_global_device_ids=true | all-gather | bytes 786432 | tf_op jit(solution)/shard_map/all_gather | solution.py:81
  49.6 0.9 reshape.244
  50.6 7.0 %all_gather.9 = bf16[4,256,256]{2,1,0:T(8,128)(2,1)S(1)} all-gather(bf16[2,256,256]{2,1,0:T(8,128)(2,1)S(1)} %bitcast.55), channel_id=1, replica_groups=mesh['dp'=4,'ctx'=2,'head'=4] {'ctx'}, dimensions={0}, use_global_device_ids=true | all-gather | bytes 786432 | tf_op jit(solution)/shard_map/all_gather | solution.py:82
  57.6 0.9 reshape.251
  58.6 3.5 %fusion.23 = (f32[512,2]{0,1:T(2,128)S(1)}, f32[512,2,128]{0,2,1:T(8,128)S(1)}) fusion(pred[512,1024]{1,0:T(8,128)(4,1)} %compare_and_fusion, bf16[1024,2,128]{2,1,0:T(2,128)(2,1)} %reshape.244, bf16[512,2,128]{2,1,0:T(2,128)(2,1)S(1)} %reshape_squeeze.11, bf16[1024,2,128]{2,1,0:T(2,128)(2,1)} %reshape.251), kind=kOutput, calls=%fused_computation.49 | convolution fusion | flops 544340992 | bytes 2363392 | tf_op jit(solution)/shard_map/while/body/eval_jaxpr/hqk,khd->qhd/dot_general | solution.py:102
  62.3 1.2 %copy.43 = f32[512,1,256]{0,2,1:T(8,128)S(1)} copy(f32[512,1,256]{2,0,1:T(8,128)} %get-tuple-element.24) | data formatting | bytes 1048576 | tf_op jit(solution)/shard_map/convert_element_type | solution.py:107
  63.5 0.8 multiply_convert_fusion.1
  64.3 2.1 %copy.40 = bf16[256,1024]{0,1:T(8,128)(2,1)} copy(bf16[256,1024]{1,0:T(8,128)(2,1)} %param.7) | data formatting | bytes 1048576 | tf_op args[3]
  66.4 3.5 %all-to-all-start.1 = ((bf16[256,4,256]{0,2,1:T(8,128)(2,1)}), bf16[256,4,256]{0,2,1:T(8,128)(2,1)S(1)}, u32[]{:S(2)}, u32[]{:S(2)}) async-start(bf16[256,4,256]{0,2,1:T(8,128)(2,1)} %bitcast.19), calls=%async_computation.1 | async-start | bytes 1048576 | tf_op jit(solution)/shard_map/all_to_all | solution.py:111
  69.9 22.0 %all-to-all-done.1 = bf16[256,4,256]{0,2,1:T(8,128)(2,1)S(1)} async-done(((bf16[256,4,256]{0,2,1:T(8,128)(2,1)}), bf16[256,4,256]{0,2,1:T(8,128)(2,1)S(1)}, u32[]{:S(2)}, u32[]{:S(2)}) %all-to-all-start.1) | async-done | bytes 524320 | tf_op jit(solution)/shard_map/all_to_all | solution.py:111
  91.9 1.0 copy.41
  93.0 4.3 %all-gather.2.cloned.1.call-done = bf16[512,1024]{0,1:T(8,128)(2,1)} async-done(((bf16[512,256]{0,1:T(8,128)(2,1)}), bf16[512,1024]{0,1:T(8,128)(2,1)}) %all-gather.2.cloned.1.call-update) | async-done | bytes 1048592 | tf_op jit(solution)/shard_map/all_gather | solution.py:113
  97.3 2.5 %fusion.6 = bf16[512,256]{1,0:T(8,128)(2,1)} fusion(f32[512,256]{1,0:T(8,128)S(1)} %bitcast.61, bf16[512,1024]{0,1:T(8,128)(2,1)} %all-gather.2.cloned.1.call-done, bf16[1024,256]{1,0:T(8,128)(2,1)} %bitcast.62), kind=kOutput, calls=%fused_computation.12 | convolution fusion | flops 268697600 | bytes 2359296 | tf_op jit(solution)/shard_map/dot_general | solution.py:112
  (26 shorter events, 0.7 us)
Async XLA Ops:
  6.5 33.7 %copy-start = (bf16[1024,4,256]{2,1,0:T(4,128)(2,1)S(1)}, bf16[1024,4,256]{2,1,0:T(4,128)(2,1)}, u32[]{:S(2)}) copy-start(bf16[1024,4,256]{2,1,0:T(4,128)(2,1)} %param.6) | copy-start | bytes 6291460
  8.4 10.1 %all-to-all-start = ((bf16[4,128,256]{2,1,0:T(8,128)(2,1)}), bf16[4,128,256]{2,1,0:T(8,128)(2,1)S(1)}, u32[]{:S(2)}, u32[]{:S(2)}) async-start(bf16[4,128,256]{2,1,0:T(8,128)(2,1)} %bitcast.2), calls=%async_computation | async-start | bytes 524288 | tf_op jit(solution)/shard_map/all_to_all | solution.py:29
  12.7 84.6 %all-gather.2.cloned.1.call-start = ((), (), s32[]{:S(2)}) async-start(), calls=%async_computation.2 | async-start | bytes 1310720 | tf_op jit(solution)/shard_map/all_gather | solution.py:113
  18.6 11.1 %collective-permute-start = (bf16[2,256,256]{2,1,0:T(8,128)(2,1)S(1)}, bf16[2,256,256]{2,1,0:T(8,128)(2,1)S(1)}, u32[]{:S(2)}, u32[]{:S(2)}) collective-permute-start(bf16[2,256,256]{2,1,0:T(8,128)(2,1)S(1)} %bitcast.58), channel_id=1, source_target_pairs={{0,1},{1,2},{2,3},{3,0},{4,5},{5,6},{6,7},{7,4},{8,9},{9,10},{10,1... | collective-permute-start | bytes 786440 | tf_op jit(solution)/shard_map/ppermute | solution.py:37
  20.5 13.7 %collective-permute-start.1 = (bf16[2,256,256]{2,1,0:T(8,128)(2,1)S(1)}, bf16[2,256,256]{2,1,0:T(8,128)(2,1)S(1)}, u32[]{:S(2)}, u32[]{:S(2)}) collective-permute-start(bf16[2,256,256]{2,1,0:T(8,128)(2,1)S(1)} %bitcast.59), channel_id=1, source_target_pairs={{0,3},{1,0},{2,1},{3,2},{4,7},{5,4},{6,5},{7,6},{8,11},{9,8},{10,9... | collective-permute-start | bytes 786440 | tf_op jit(solution)/shard_map/ppermute | solution.py:40
  29.7 9.5 %collective-permute-start.2 = (bf16[2,256,256]{2,1,0:T(8,128)(2,1)S(1)}, bf16[2,256,256]{2,1,0:T(8,128)(2,1)S(1)}, u32[]{:S(2)}, u32[]{:S(2)}) collective-permute-start(bf16[2,256,256]{2,1,0:T(8,128)(2,1)S(1)} %collective-permute-done), channel_id=1, source_target_pairs={{0,1},{1,2},{2,3},{3,0},{4,5},{5,6},{6,7},{7,4},{8,9},{9,10},{10,1... | collective-permute-start | bytes 786440 | tf_op jit(solution)/shard_map/ppermute | solution.py:37
  66.4 25.5 %all-to-all-start.1 = ((bf16[256,4,256]{0,2,1:T(8,128)(2,1)}), bf16[256,4,256]{0,2,1:T(8,128)(2,1)S(1)}, u32[]{:S(2)}, u32[]{:S(2)}) async-start(bf16[256,4,256]{0,2,1:T(8,128)(2,1)} %bitcast.19), calls=%async_computation.1 | async-start | bytes 1048576 | tf_op jit(solution)/shard_map/all_to_all | solution.py:111
Sparse Core Ops, SparseCore 0:
  64.5 32.8 all-gather.1
